TPU v7x, 32 devices: a whole 2x2x4 slice. The times are simulated.
32 devices in a mesh: lsec: 4 (over y, x), rsec: 8 (over z, core).
Axes of the slice: x: 2, y: 2, z: 4, core: 2. Of those that a mesh axis runs over, the one named last changes fastest.
Arguments:
- psi: bfloat16 [16, 16, 256, 256], P('lsec', 'rsec'), may hold values from -6 to 6
- left_env: bfloat16 [16, 4, 256, 256], P('lsec'), may hold values from -0.375 to 0.375
- right_env: bfloat16 [16, 4, 256, 256], P('rsec'), may hold values from -0.1875 to 0.1875
- energies: float32 [16, 16], P('lsec', 'rsec'), may hold values from 0.5 to 3
- coef_num: int32 [2], replicated, may hold values from 3 to 9
- coef_den: int32 [2], replicated, may hold values from 4 to 8
Outputs:
- vector_out: bfloat16 [16, 16, 256, 256], P('lsec', 'rsec')
- ritz: float32 [3], replicated
All inputs are finite; a program needn't handle non-finite values.
Results may differ from a plain program's by a relative error of at most 0.015.
Values may be sent and summed in bfloat16 or wider, within the bound.
A program may use at most 64 MiB of HBM per device.

v0:
```python
import jax
import jax.numpy as jnp
from jax import lax
from jax.sharding import PartitionSpec as P

DIAG = 2
HOPS = 1
ITERS = 3
eps = 1e-06


def padded(block, sides, width):
    for axis, dim in sides:
        count = lax.axis_size(axis)
        forward = [(i, i + 1) for i in range(count - 1)]
        backward = [(target, source) for source, target in forward]
        low = lax.ppermute(
            lax.slice_in_dim(block, block.shape[dim] - width, None, axis=dim), axis, forward
        )
        high = lax.ppermute(lax.slice_in_dim(block, 0, width, axis=dim), axis, backward)
        block = jnp.concatenate([low, block, high], axis=dim)
    return block


def add_terms(left_env, right_env, source, first, number, total):
    for term in range(first, first + number):
        inner = jnp.einsum(
            "aij,abjk->abik", left_env[:, term], source, preferred_element_type=jnp.float32
        ).astype(jnp.bfloat16)
        total = total + jnp.einsum(
            "abik,blk->abil", inner, right_env[:, term], preferred_element_type=jnp.float32
        )
    return total


def with_rims(vec):
    wide = padded(vec, (("rsec", 1),), 1)
    full = padded(wide, (("lsec", 0),), 1)
    return full


def matvec(vec, left_env, right_env, energies):
    vals = vec.astype(jnp.float32)
    total = energies[:, :, None, None] * vals
    total = add_terms(left_env, right_env, vec, 0, DIAG, total)
    full = with_rims(vec)
    plus_blocks = full[:-2, 2:]
    minus_blocks = full[2:, :-2]
    total = add_terms(left_env, right_env, plus_blocks, DIAG, HOPS, total)
    total = add_terms(left_env, right_env, minus_blocks, DIAG + HOPS, HOPS, total)
    return total


def per_device(psi, left_env, right_env, energies, coef_num, coef_den):
    count = 1.0 / float(psi.size * lax.axis_size("lsec") * lax.axis_size("rsec"))
    start_vals = psi.astype(jnp.float32)
    start = lax.psum(jnp.sum(start_vals * start_vals), ("lsec", "rsec")) * count
    vec = (start_vals * lax.rsqrt(start + eps)).astype(jnp.bfloat16)
    previous = jnp.zeros(psi.shape, jnp.float32)
    thetas = []
    for step in range(ITERS):
        sigma = matvec(vec, left_env, right_env, energies)
        vals = vec.astype(jnp.float32)
        if step == 0:
            coef = jnp.float32(0.0)
        else:
            coef = coef_num[step - 1].astype(jnp.float32) / coef_den[step - 1].astype(jnp.float32)
        sums = lax.psum(
            (
                jnp.sum(sigma * sigma),
                jnp.sum(sigma * vals),
                jnp.sum(sigma * previous),
                jnp.sum(vals * vals),
                jnp.sum(vals * previous),
                jnp.sum(previous * previous),
            ),
            ("lsec", "rsec"),
        )
        m_ss, m_sv, m_sp, m_vv, m_vp, m_pp = [part * count for part in sums]
        resid = sigma - m_sv * vals - coef * previous
        norm_sq = (
            m_ss
            - 2.0 * m_sv * m_sv
            - 2.0 * coef * m_sp
            + m_sv * m_sv * m_vv
            + 2.0 * m_sv * coef * m_vp
            + coef * coef * m_pp
        )
        thetas.append(m_sv)
        previous = vals
        vec = (resid * lax.rsqrt(norm_sq + eps)).astype(jnp.bfloat16)
    return (vec, jnp.stack(thetas))


def solution(mesh):
    in_specs = (
        P("lsec", "rsec", None, None),
        P("lsec", None, None, None),
        P("rsec", None, None, None),
        P("lsec", "rsec"),
        P(),
        P(),
    )
    out_specs = (P("lsec", "rsec", None, None), P())
    return jax.shard_map(
        per_device, mesh=mesh, in_specs=in_specs, out_specs=out_specs, check_vma=False
    )
```

profile of v0, /device:TPU:0, one launch (start us, length us, event | category | flops | bytes accessed | tf_op | source)
XLA Modules:
  0.0 343.5 jit_solution(12554492794385849762)
XLA Ops:
  0.6 2.4 fusion
  3.0 42.2 %psum.125 = f32[]{:T(128)} all-reduce(f32[]{:T(128)} %fusion), channel_id=1, replica_groups=mesh['lsec'=4,'rsec'=8] {'lsec','rsec'}, use_global_device_ids=true, to_apply=%region_1.0 | all-reduce | flops 1 | bytes 8 | tf_op jit(solution)/shard_map/psum | solution.py:57
  47.4 1.5 collective-permute-start
  50.3 4.0 %collective-permute-done.1 = bf16[4,1,256,256]{3,2,0,1:T(8,128)(2,1)S(1)} collective-permute-done((bf16[4,1,256,256]{3,2,0,1:T(8,128)(2,1)S(1)}, bf16[4,1,256,256]{3,2,0,1:T(8,128)(2,1)S(1)}, u32[]{:S(2)}, u32[]{:S(2)}) %collective-permute-start.1) | collective-permute-done | bytes 524320 | tf_op jit(solution)/shard_map/ppermute | solution.py:20
  55.5 5.0 %collective-permute-start.2 = (bf16[1,4,256,256]{3,2,0,1:T(8,128)(2,1)}, bf16[1,4,256,256]{3,2,0,1:T(8,128)(2,1)}, u32[]{:S(2)}, u32[]{:S(2)}) collective-permute-start(bf16[1,4,256,256]{3,2,0,1:T(8,128)(2,1)} %get-tuple-element.40), channel_id=1, source_target_pairs={{0,8},{8,16},{16,24},{1,9},{9,17},{17,25},{2,10},{10,18},{18,26},{... | collective-permute-start | bytes 1572872 | tf_op jit(solution)/shard_map/ppermute | solution.py:17
  60.5 3.0 fusion.37
  64.7 3.0 fusion.39
  67.8 3.2 fusion.41
  71.0 9.3 %collective-permute-done.3 = bf16[1,4,256,256]{3,2,0,1:T(8,128)(2,1)} collective-permute-done((bf16[1,4,256,256]{3,2,0,1:T(8,128)(2,1)}, bf16[1,4,256,256]{3,2,0,1:T(8,128)(2,1)}, u32[]{:S(2)}, u32[]{:S(2)}) %collective-permute-start.3) | collective-permute-done | bytes 524320 | tf_op jit(solution)/shard_map/ppermute | solution.py:20
  80.3 6.9 %multiply_reduce_fusion.2 = (f32[]{:T(128)}, f32[]{:T(128)}, f32[]{:T(128)}, f32[]{:T(128)}, f32[]{:T(128)}, /*index=5*/f32[4,2,256,256]{3,2,0,1:T(8,128)}) fusion(bf16[4,2,256,256]{3,2,0,1:T(8,128)(2,1)S(1)} %fusion.1, bf16[2,4,256,256]{3,2,1,0:T(8,128)(2,1)} %param.8, bf16[1,4,256,256]{3,2,0,1:T(8,128)(2,1)} %collective-permute-done.3, ...), kind=kOutput, calls=%fused_computation.59 | convolution fusion | flops 549978112 | bytes 12846100 | tf_op jit(solution)/shard_map/abik,blk->abil/dot_general | solution.py:30
  87.2 50.7 %all-reduce.2 = (f32[]{:T(128)}, f32[]{:T(128)}, f32[]{:T(128)}, f32[]{:T(128)}, f32[]{:T(128)}, /*index=5*/f32[]{:T(128)}) all-reduce(f32[]{:T(128)} %get-tuple-element.13, f32[]{:T(128)} %get-tuple-element.14, f32[]{:T(128)} %get-tuple-element.12, f32[]{:T(128)} %get-tuple-element.16, ...), channel_id=1, replica_groups=mesh['lsec'=4,'rsec'=8] {'lsec','rsec'}, use_global_device_ids=true, to_apply=%region_5.0 | all-reduce | flops 6 | bytes 48 | tf_op jit(solution)/shard_map/psum | solution.py:68
  143.8 2.0 fusion.19
  146.9 2.1 collective-permute-start.4
  153.5 2.2 pad_maximum_fusion.57
  155.6 5.0 %collective-permute-start.6 = (bf16[1,4,256,256]{3,2,0,1:T(8,128)(2,1)}, bf16[1,4,256,256]{3,2,0,1:T(8,128)(2,1)}, u32[]{:S(2)}, u32[]{:S(2)}) collective-permute-start(bf16[1,4,256,256]{3,2,0,1:T(8,128)(2,1)} %get-tuple-element.38), channel_id=1, source_target_pairs={{0,8},{8,16},{16,24},{1,9},{9,17},{17,25},{2,10},{10,18},{18,26},{... | collective-permute-start | bytes 1572872 | tf_op jit(solution)/shard_map/ppermute | solution.py:17
  160.6 3.1 fusion.44
  165.0 3.2 fusion.46
  168.2 3.3 fusion.48
  171.6 9.2 %collective-permute-done.7 = bf16[1,4,256,256]{3,2,0,1:T(8,128)(2,1)} collective-permute-done((bf16[1,4,256,256]{3,2,0,1:T(8,128)(2,1)}, bf16[1,4,256,256]{3,2,0,1:T(8,128)(2,1)}, u32[]{:S(2)}, u32[]{:S(2)}) %collective-permute-start.7) | collective-permute-done | bytes 524320 | tf_op jit(solution)/shard_map/ppermute | solution.py:20
  180.7 7.0 %fusion.25 = (f32[]{:T(128)}, f32[]{:T(128)}, f32[]{:T(128)}, f32[]{:T(128)}, f32[]{:T(128)}, /*index=5*/f32[4,2,256,256]{3,2,0,1:T(8,128)}) fusion(bf16[4,2,256,256]{3,2,0,1:T(8,128)(2,1)S(1)} %fusion.1, bf16[4,2,256,256]{3,2,0,1:T(8,128)(2,1)S(1)} %fusion.19, bf16[2,4,256,256]{3,2,1,0:T(8,128)(2,1)} %param.8, ...), kind=kOutput, calls=%fused_computation.46 | convolution fusion | flops 550502400 | bytes 13894676 | tf_op jit(solution)/shard_map/abik,blk->abil/dot_general | solution.py:30
  187.8 48.5 %all-reduce.1 = (f32[]{:T(128)}, f32[]{:T(128)}, f32[]{:T(128)}, f32[]{:T(128)}, f32[]{:T(128)}) all-reduce(f32[]{:T(128)} %get-tuple-element.9, f32[]{:T(128)} %get-tuple-element.10, f32[]{:T(128)} %get-tuple-element.8, f32[]{:T(128)} %get-tuple-element.17, f32[]{:T(128)} %get-tuple-element.11), channel_id=1, replica_groups=mesh['lsec'=4,'rsec'=8] {'lsec','rsec'}, use_global_device_ids=true, to_apply=%region_16.0 | all-reduce | flops 5 | bytes 40 | tf_op jit(solution)/shard_map/psum | solution.py:68
  241.2 2.2 fusion.24
  244.4 2.2 collective-permute-start.8
  250.8 2.2 pad_maximum_fusion.54
  253.0 5.0 %collective-permute-start.10 = (bf16[1,4,256,256]{3,2,0,1:T(8,128)(2,1)}, bf16[1,4,256,256]{3,2,0,1:T(8,128)(2,1)}, u32[]{:S(2)}, u32[]{:S(2)}) collective-permute-start(bf16[1,4,256,256]{3,2,0,1:T(8,128)(2,1)} %get-tuple-element.36), channel_id=1, source_target_pairs={{0,8},{8,16},{16,24},{1,9},{9,17},{17,25},{2,10},{10,18},{18,26},{... | collective-permute-start | bytes 1572872 | tf_op jit(solution)/shard_map/ppermute | solution.py:17
  257.9 3.0 fusion.51
  262.3 3.1 fusion.53
  265.4 3.3 fusion.55
  268.7 9.3 %collective-permute-done.11 = bf16[1,4,256,256]{3,2,0,1:T(8,128)(2,1)} collective-permute-done((bf16[1,4,256,256]{3,2,0,1:T(8,128)(2,1)}, bf16[1,4,256,256]{3,2,0,1:T(8,128)(2,1)}, u32[]{:S(2)}, u32[]{:S(2)}) %collective-permute-start.11) | collective-permute-done | bytes 524320 | tf_op jit(solution)/shard_map/ppermute | solution.py:20
  278.0 6.9 %fusion.34 = (f32[]{:T(128)}, f32[]{:T(128)}, f32[]{:T(128)}, f32[]{:T(128)}, f32[]{:T(128)}, /*index=5*/f32[4,2,256,256]{3,2,0,1:T(8,128)}) fusion(bf16[4,2,256,256]{3,2,0,1:T(8,128)(2,1)S(1)} %fusion.19, bf16[4,2,256,256]{3,2,0,1:T(8,128)(2,1)S(1)} %fusion.24, bf16[2,4,256,256]{3,2,1,0:T(8,128)(2,1)S(1)} %copy-done.2, ...), kind=kOutput, calls=%fused_computation.55 | convolution fusion | flops 550502400 | bytes 13894676 | tf_op jit(solution)/shard_map/abik,blk->abil/dot_general | solution.py:30
  284.9 49.4 %all-reduce = (f32[]{:T(128)}, f32[]{:T(128)}, f32[]{:T(128)}, f32[]{:T(128)}, f32[]{:T(128)}) all-reduce(f32[]{:T(128)} %get-tuple-element.5, f32[]{:T(128)} %get-tuple-element.6, f32[]{:T(128)} %get-tuple-element.4, f32[]{:T(128)} %get-tuple-element.18, f32[]{:T(128)} %get-tuple-element.7), channel_id=1, replica_groups=mesh['lsec'=4,'rsec'=8] {'lsec','rsec'}, use_global_device_ids=true, to_apply=%region_26.0 | all-reduce | flops 5 | bytes 40 | tf_op jit(solution)/shard_map/psum | solution.py:68
  339.7 2.1 fusion.10
  (39 shorter events, 16.3 us)
Async XLA Ops:
  47.4 13.1 %copy-start.1 = (bf16[4,4,256,256]{3,2,1,0:T(8,128)(2,1)S(1)}, bf16[4,4,256,256]{3,2,1,0:T(8,128)(2,1)}, u32[]{:S(2)}) copy-start(bf16[4,4,256,256]{3,2,1,0:T(8,128)(2,1)} %param.7) | copy-start | bytes 6291460
  47.4 2.9 collective-permute-start
  48.8 5.5 %collective-permute-start.1 = (bf16[4,1,256,256]{3,2,0,1:T(8,128)(2,1)S(1)}, bf16[4,1,256,256]{3,2,0,1:T(8,128)(2,1)S(1)}, u32[]{:S(2)}, u32[]{:S(2)}) collective-permute-start(bf16[4,1,256,256]{3,2,0,1:T(8,128)(2,1)S(1)} %get-tuple-element.46), channel_id=1, source_target_pairs={{1,0},{2,1},{3,2},{4,3},{5,4},{6,5},{7,6},{9,8},{10,9},{11,10},{12... | collective-permute-start | bytes 1572872 | tf_op jit(solution)/shard_map/ppermute | solution.py:20
  50.3 4.0 %copy-start.3 = (bf16[4,1,256,256]{3,2,0,1:T(8,128)(2,1)}, bf16[4,1,256,256]{3,2,0,1:T(8,128)(2,1)S(1)}, u32[]{:S(2)}) copy-start(bf16[4,1,256,256]{3,2,0,1:T(8,128)(2,1)S(1)} %collective-permute-done) | copy-start | bytes 1572868
  54.3 1.1 copy-start.4
  55.5 12.3 %collective-permute-start.2 = (bf16[1,4,256,256]{3,2,0,1:T(8,128)(2,1)}, bf16[1,4,256,256]{3,2,0,1:T(8,128)(2,1)}, u32[]{:S(2)}, u32[]{:S(2)}) collective-permute-start(bf16[1,4,256,256]{3,2,0,1:T(8,128)(2,1)} %get-tuple-element.40), channel_id=1, source_target_pairs={{0,8},{8,16},{16,24},{1,9},{9,17},{17,25},{2,10},{10,18},{18,26},{... | collective-permute-start | bytes 1572872 | tf_op jit(solution)/shard_map/ppermute | solution.py:17
  63.4 16.8 %collective-permute-start.3 = (bf16[1,4,256,256]{3,2,0,1:T(8,128)(2,1)}, bf16[1,4,256,256]{3,2,0,1:T(8,128)(2,1)}, u32[]{:S(2)}, u32[]{:S(2)}) collective-permute-start(bf16[1,4,256,256]{3,2,0,1:T(8,128)(2,1)} %get-tuple-element.39), channel_id=1, source_target_pairs={{8,0},{16,8},{24,16},{9,1},{17,9},{25,17},{10,2},{18,10},{26,18},{... | collective-permute-start | bytes 1572872 | tf_op jit(solution)/shard_map/ppermute | solution.py:20
  67.7 12.5 %copy-start.7 = (f32[4,2]{0,1:T(2,128)S(1)}, f32[4,2]{0,1:T(2,128)}, u32[]{:S(2)}) copy-start(f32[4,2]{0,1:T(2,128)} %param.9) | copy-start | bytes 100
  71.0 72.9 %copy-start = (bf16[4,2,256,256]{3,2,1,0:T(8,128)(2,1)S(1)}, bf16[4,2,256,256]{3,2,1,0:T(8,128)(2,1)}, u32[]{:S(2)}) copy-start(bf16[4,2,256,256]{3,2,1,0:T(8,128)(2,1)} %param.6) | copy-start | bytes 3145732
  145.8 4.5 %copy-start.5 = (s32[2]{0:T(128)S(1)}, s32[2]{0:T(128)}, u32[]{:S(2)}) copy-start(s32[2]{0:T(128)} %param.10) | copy-start | bytes 28
  145.8 5.7 %copy-start.6 = (s32[2]{0:T(128)S(1)}, s32[2]{0:T(128)}, u32[]{:S(2)}) copy-start(s32[2]{0:T(128)} %param.11) | copy-start | bytes 28
  146.9 6.6 %collective-permute-start.4 = (bf16[4,1,256,256]{3,2,0,1:T(8,128)(2,1)}, bf16[4,1,256,256]{3,2,0,1:T(8,128)(2,1)}, u32[]{:S(2)}, u32[]{:S(2)}) collective-permute-start(bf16[4,1,256,256]{3,2,0,1:T(8,128)(2,1)} %get-tuple-element.43), channel_id=1, source_target_pairs={{0,1},{1,2},{2,3},{3,4},{4,5},{5,6},{6,7},{8,9},{9,10},{10,11},{11... | collective-permute-start | bytes 1572872 | tf_op jit(solution)/shard_map/ppermute | solution.py:17
  149.0 4.5 %collective-permute-start.5 = (bf16[4,1,256,256]{3,2,0,1:T(8,128)(2,1)}, bf16[4,1,256,256]{3,2,0,1:T(8,128)(2,1)}, u32[]{:S(2)}, u32[]{:S(2)}) collective-permute-start(bf16[4,1,256,256]{3,2,0,1:T(8,128)(2,1)} %get-tuple-element.44), channel_id=1, source_target_pairs={{1,0},{2,1},{3,2},{4,3},{5,4},{6,5},{7,6},{9,8},{10,9},{11,10},{12... | collective-permute-start | bytes 1572872 | tf_op jit(solution)/shard_map/ppermute | solution.py:20
  155.6 12.6 %collective-permute-start.6 = (bf16[1,4,256,256]{3,2,0,1:T(8,128)(2,1)}, bf16[1,4,256,256]{3,2,0,1:T(8,128)(2,1)}, u32[]{:S(2)}, u32[]{:S(2)}) collective-permute-start(bf16[1,4,256,256]{3,2,0,1:T(8,128)(2,1)} %get-tuple-element.38), channel_id=1, source_target_pairs={{0,8},{8,16},{16,24},{1,9},{9,17},{17,25},{2,10},{10,18},{18,26},{... | collective-permute-start | bytes 1572872 | tf_op jit(solution)/shard_map/ppermute | solution.py:17
  163.8 17.0 %collective-permute-start.7 = (bf16[1,4,256,256]{3,2,0,1:T(8,128)(2,1)}, bf16[1,4,256,256]{3,2,0,1:T(8,128)(2,1)}, u32[]{:S(2)}, u32[]{:S(2)}) collective-permute-start(bf16[1,4,256,256]{3,2,0,1:T(8,128)(2,1)} %get-tuple-element.37), channel_id=1, source_target_pairs={{8,0},{16,8},{24,16},{9,1},{17,9},{25,17},{10,2},{18,10},{26,18},{... | collective-permute-start | bytes 1572872 | tf_op jit(solution)/shard_map/ppermute | solution.py:20
  244.4 13.5 %copy-start.2 = (bf16[2,4,256,256]{3,2,1,0:T(8,128)(2,1)S(1)}, bf16[2,4,256,256]{3,2,1,0:T(8,128)(2,1)}, u32[]{:S(2)}) copy-start(bf16[2,4,256,256]{3,2,1,0:T(8,128)(2,1)} %param.8) | copy-start | bytes 3145732
  244.4 5.5 %collective-permute-start.8 = (bf16[4,1,256,256]{3,2,0,1:T(8,128)(2,1)}, bf16[4,1,256,256]{3,2,0,1:T(8,128)(2,1)}, u32[]{:S(2)}, u32[]{:S(2)}) collective-permute-start(bf16[4,1,256,256]{3,2,0,1:T(8,128)(2,1)} %get-tuple-element.41), channel_id=1, source_target_pairs={{0,1},{1,2},{2,3},{3,4},{4,5},{5,6},{6,7},{8,9},{9,10},{10,11},{11... | collective-permute-start | bytes 1572872 | tf_op jit(solution)/shard_map/ppermute | solution.py:17
  246.6 4.1 %collective-permute-start.9 = (bf16[4,1,256,256]{3,2,0,1:T(8,128)(2,1)}, bf16[4,1,256,256]{3,2,0,1:T(8,128)(2,1)}, u32[]{:S(2)}, u32[]{:S(2)}) collective-permute-start(bf16[4,1,256,256]{3,2,0,1:T(8,128)(2,1)} %get-tuple-element.42), channel_id=1, source_target_pairs={{1,0},{2,1},{3,2},{4,3},{5,4},{6,5},{7,6},{9,8},{10,9},{11,10},{12... | collective-permute-start | bytes 1572872 | tf_op jit(solution)/shard_map/ppermute | solution.py:20
  253.0 12.4 %collective-permute-start.10 = (bf16[1,4,256,256]{3,2,0,1:T(8,128)(2,1)}, bf16[1,4,256,256]{3,2,0,1:T(8,128)(2,1)}, u32[]{:S(2)}, u32[]{:S(2)}) collective-permute-start(bf16[1,4,256,256]{3,2,0,1:T(8,128)(2,1)} %get-tuple-element.36), channel_id=1, source_target_pairs={{0,8},{8,16},{16,24},{1,9},{9,17},{17,25},{2,10},{10,18},{18,26},{... | collective-permute-start | bytes 1572872 | tf_op jit(solution)/shard_map/ppermute | solution.py:17
  261.0 17.0 %collective-permute-start.11 = (bf16[1,4,256,256]{3,2,0,1:T(8,128)(2,1)}, bf16[1,4,256,256]{3,2,0,1:T(8,128)(2,1)}, u32[]{:S(2)}, u32[]{:S(2)}) collective-permute-start(bf16[1,4,256,256]{3,2,0,1:T(8,128)(2,1)} %get-tuple-element.35), channel_id=1, source_target_pairs={{8,0},{16,8},{24,16},{9,1},{17,9},{25,17},{10,2},{18,10},{26,18},{... | collective-permute-start | bytes 1572872 | tf_op jit(solution)/shard_map/ppermute | solution.py:20
where the time goes:
time: 345 us; the launch traced here: 343 us
  blocking collectives  191 us (55%)
  matrix products  49.2 us (14%)
  waiting for transfers between devices  32.9 us (10%)
  starting transfers between devices  28.5 us (8%)
  between operations  21.7 us (6%)
  other arithmetic  16.1 us (5%)
  local copies, waits for them, and re-layouts  4.39 us (1%)
    psum x3, blocking collectives, per_device(): lax.psum((jnp.sum(sigma * sigma), jnp.sum(sigma * vals), jnp.sum(sigma *...  149 us
    dot_general x12, matrix products, add_terms(): jnp.einsum('abik,blk->abil', inner, right_env[:, term], preferred_element...  49.2 us
    psum x1, blocking collectives, per_device(): start = lax.psum(jnp.sum(start_vals * start_vals), ('lsec', 'rsec')) * count  42.2 us
    ppermute x6, waiting for transfers between devices, padded(): lax.ppermute(lax.slice_in_dim(block, 0, width, axis=dim), axis, backward)  32.7 us
    ppermute x6, starting transfers between devices, padded(): lax.ppermute(lax.slice_in_dim(block, block.shape[dim] - width, None, axis...  20.8 us
    ppermute x6, starting transfers between devices, padded(): lax.ppermute(lax.slice_in_dim(block, 0, width, axis=dim), axis, backward)  7.69 us
  transfers between devices with their start and end apart: 12, of which 6 were waited for; matrix products, arithmetic and copies ran while one was open for 9% of the time, Pallas kernels for 0%

commit v1 on v0

--- a/solution.py
+++ b/solution.py
@@ -65,17 +65,16 @@
             coef = jnp.float32(0.0)
         else:
             coef = coef_num[step - 1].astype(jnp.float32) / coef_den[step - 1].astype(jnp.float32)
-        sums = lax.psum(
-            (
-                jnp.sum(sigma * sigma),
-                jnp.sum(sigma * vals),
-                jnp.sum(sigma * previous),
-                jnp.sum(vals * vals),
-                jnp.sum(vals * previous),
-                jnp.sum(previous * previous),
-            ),
-            ("lsec", "rsec"),
+        sums = (
+            jnp.sum(sigma * sigma),
+            jnp.sum(sigma * vals),
+            jnp.sum(sigma * previous),
+            jnp.sum(vals * vals),
+            jnp.sum(vals * previous),
+            jnp.sum(previous * previous),
         )
+        for over in ("rsec", "lsec"):
+            sums = lax.psum(sums, over)
         m_ss, m_sv, m_sp, m_vv, m_vp, m_pp = [part * count for part in sums]
         resid = sigma - m_sv * vals - coef * previous
         norm_sq = (

time: 345 us -> 289 us (0.84)
  blocking collectives: 191 us -> 136 us
    psum x3 -> x6, blocking collectives: 149 us -> 94 us  [per_device(): sums = lax.psum(sums, over)]
  transfers between devices with their start and end apart: 12 -> 12, of which waited for: 6 -> 6; matrix products, arithmetic and copies ran while one was open for 9% -> 10% of each run, Pallas kernels for 0% -> 0%
where the time goes in v1:
time: 289 us; the launch traced here: 288 us
  blocking collectives  136 us (47%)
  matrix products  49.2 us (17%)
  waiting for transfers between devices  33.7 us (12%)
  starting transfers between devices  26.7 us (9%)
  between operations  21.6 us (7%)
  other arithmetic  16.1 us (6%)
  local copies, waits for them, and re-layouts  4.39 us (2%)
    psum x6, blocking collectives, per_device(): sums = lax.psum(sums, over)  94 us
    dot_general x12, matrix products, add_terms(): jnp.einsum('abik,blk->abil', inner, right_env[:, term], preferred_element...  49.2 us
    psum x1, blocking collectives, per_device(): start = lax.psum(jnp.sum(start_vals * start_vals), ('lsec', 'rsec')) * count  42.2 us
    ppermute x6, waiting for transfers between devices, padded(): lax.ppermute(lax.slice_in_dim(block, 0, width, axis=dim), axis, backward)  33.5 us
    ppermute x6, starting transfers between devices, padded(): lax.ppermute(lax.slice_in_dim(block, block.shape[dim] - width, None, axis...  19 us
    ppermute x6, starting transfers between devices, padded(): lax.ppermute(lax.slice_in_dim(block, 0, width, axis=dim), axis, backward)  7.69 us
    convert_element_type x3, other arithmetic, per_device(): vec = (resid * lax.rsqrt(norm_sq + eps)).astype(jnp.bfloat16)  6.25 us
  transfers between devices with their start and end apart: 12, of which 6 were waited for; matrix products, arithmetic and copies ran while one was open for 10% of the time, Pallas kernels for 0%

profile of v1, /device:TPU:0, one launch (start us, length us, event | category | flops | bytes accessed | tf_op | source)
XLA Modules:
  0.0 287.8 jit_solution(6876270962718620609)
XLA Ops:
  0.6 2.4 fusion
  3.0 42.2 %psum.243 = f32[]{:T(128)} all-reduce(f32[]{:T(128)} %fusion), channel_id=1, replica_groups=mesh['lsec'=4,'rsec'=8] {'lsec','rsec'}, use_global_device_ids=true, to_apply=%region_1.0 | all-reduce | flops 1 | bytes 8 | tf_op jit(solution)/shard_map/psum | solution.py:57
  50.3 4.0 %collective-permute-done.1 = bf16[4,1,256,256]{3,2,0,1:T(8,128)(2,1)S(1)} collective-permute-done((bf16[4,1,256,256]{3,2,0,1:T(8,128)(2,1)S(1)}, bf16[4,1,256,256]{3,2,0,1:T(8,128)(2,1)S(1)}, u32[]{:S(2)}, u32[]{:S(2)}) %collective-permute-start.1) | collective-permute-done | bytes 524320 | tf_op jit(solution)/shard_map/ppermute | solution.py:20
  55.5 5.0 %collective-permute-start.2 = (bf16[1,4,256,256]{3,2,0,1:T(8,128)(2,1)}, bf16[1,4,256,256]{3,2,0,1:T(8,128)(2,1)}, u32[]{:S(2)}, u32[]{:S(2)}) collective-permute-start(bf16[1,4,256,256]{3,2,0,1:T(8,128)(2,1)} %get-tuple-element.56), channel_id=1, source_target_pairs={{0,8},{8,16},{16,24},{1,9},{9,17},{17,25},{2,10},{10,18},{18,26},{... | collective-permute-start | bytes 1572872 | tf_op jit(solution)/shard_map/ppermute | solution.py:17
  60.5 3.0 %fusion.37 = f32[2,4,256,256]{3,2,1,0:T(8,128)} fusion(bf16[4,2,256,256]{3,2,0,1:T(8,128)(2,1)S(1)} %fusion.1, bf16[4,4,256,256]{3,2,1,0:T(8,128)(2,1)S(1)} %copy-done.1, bf16[2,4,256,256]{3,2,1,0:T(8,128)(2,1)} %param.8), kind=kOutput, calls=%fused_computation.74 | convolution fusion | flops 537395200 | bytes 3932160 | tf_op jit(solution)/shard_map/abik,blk->abil/dot_general | solution.py:30
  64.7 3.0 %fusion.39 = f32[2,4,256,256]{3,2,1,0:T(8,128)} fusion(bf16[4,2,256,256]{3,2,0,1:T(8,128)(2,1)S(1)} %fusion.1, bf16[4,4,256,256]{3,2,1,0:T(8,128)(2,1)S(1)} %copy-done.1, bf16[2,4,256,256]{3,2,1,0:T(8,128)(2,1)} %param.8), kind=kOutput, calls=%fused_computation.76 | convolution fusion | flops 537395200 | bytes 3932160 | tf_op jit(solution)/shard_map/abik,blk->abil/dot_general | solution.py:30
  67.7 3.2 %fusion.41 = f32[2,4,256,256]{3,2,1,0:T(8,128)} fusion(bf16[1,4,256,256]{3,2,0,1:T(8,128)(2,1)} %collective-permute-done.2, bf16[4,1,256,256]{3,2,0,1:T(8,128)(2,1)} %copy-done.4, bf16[4,2,256,256]{3,2,0,1:T(8,128)(2,1)S(1)} %fusion.1, bf16[4,1,256,256]{3,2,0,1:T(8,128)(2,1)} %copy-done.3, bf16[4,4,256,256]{3,2,1,0:T(8,128)(2,1)S(1)} %copy-done.1, ...), kind=kOutput, calls=%fused_computation.78 | convolution fusion | flops 541589504 | bytes 5505024 | tf_op jit(solution)/shard_map/abik,blk->abil/dot_general | solution.py:30
  70.9 9.3 %collective-permute-done.3 = bf16[1,4,256,256]{3,2,0,1:T(8,128)(2,1)} collective-permute-done((bf16[1,4,256,256]{3,2,0,1:T(8,128)(2,1)}, bf16[1,4,256,256]{3,2,0,1:T(8,128)(2,1)}, u32[]{:S(2)}, u32[]{:S(2)}) %collective-permute-start.3) | collective-permute-done | bytes 524320 | tf_op jit(solution)/shard_map/ppermute | solution.py:20
  80.2 6.9 %multiply_reduce_fusion.2 = (f32[]{:T(128)}, f32[]{:T(128)}, f32[]{:T(128)}, f32[]{:T(128)}, f32[]{:T(128)}, /*index=5*/f32[4,2,256,256]{3,2,0,1:T(8,128)}) fusion(bf16[4,2,256,256]{3,2,0,1:T(8,128)(2,1)S(1)} %fusion.1, bf16[2,4,256,256]{3,2,1,0:T(8,128)(2,1)} %param.8, bf16[1,4,256,256]{3,2,0,1:T(8,128)(2,1)} %collective-permute-done.3, ...), kind=kOutput, calls=%fused_computation.59 | convolution fusion | flops 549978112 | bytes 12846100 | tf_op jit(solution)/shard_map/abik,blk->abil/dot_general | solution.py:30
  87.2 24.5 %all-reduce.2 = (f32[]{:T(128)}, f32[]{:T(128)}, f32[]{:T(128)}, f32[]{:T(128)}, f32[]{:T(128)}, /*index=5*/f32[]{:T(128)}) all-reduce(f32[]{:T(128)} %get-tuple-element.13, f32[]{:T(128)} %get-tuple-element.14, f32[]{:T(128)} %get-tuple-element.12, f32[]{:T(128)} %get-tuple-element.16, ...), channel_id=1, replica_groups=mesh['lsec'=4,'rsec'=8] {'rsec'}, use_global_device_ids=true, to_apply=%region_6.0 | all-reduce | flops 6 | bytes 48 | tf_op jit(solution)/shard_map/psum | solution.py:77
  111.7 8.7 %all-reduce.5 = (f32[]{:T(128)}, f32[]{:T(128)}, f32[]{:T(128)}, f32[]{:T(128)}, f32[]{:T(128)}, /*index=5*/f32[]{:T(128)}) all-reduce(f32[]{:T(128)} %get-tuple-element.29, f32[]{:T(128)} %get-tuple-element.30, f32[]{:T(128)} %get-tuple-element.31, f32[]{:T(128)} %get-tuple-element.32, ...), channel_id=1, replica_groups=mesh['lsec'=4,'rsec'=8] {'lsec'}, use_global_device_ids=true, to_apply=%region_7.0 | all-reduce | flops 6 | bytes 48 | tf_op jit(solution)/shard_map/psum | solution.py:77
  129.1 2.1 collective-permute-start.4
  135.7 2.2 pad_maximum_fusion.57
  137.9 4.1 %collective-permute-start.6 = (bf16[1,4,256,256]{3,2,0,1:T(8,128)(2,1)}, bf16[1,4,256,256]{3,2,0,1:T(8,128)(2,1)}, u32[]{:S(2)}, u32[]{:S(2)}) collective-permute-start(bf16[1,4,256,256]{3,2,0,1:T(8,128)(2,1)} %get-tuple-element.54), channel_id=1, source_target_pairs={{0,8},{8,16},{16,24},{1,9},{9,17},{17,25},{2,10},{10,18},{18,26},{... | collective-permute-start | bytes 1572872 | tf_op jit(solution)/shard_map/ppermute | solution.py:17
  142.0 3.1 %fusion.44 = f32[2,4,256,256]{3,2,1,0:T(8,128)} fusion(bf16[4,2,256,256]{3,2,0,1:T(8,128)(2,1)S(1)} %fusion.19, bf16[4,4,256,256]{3,2,1,0:T(8,128)(2,1)} %param.7, bf16[2,4,256,256]{3,2,1,0:T(8,128)(2,1)} %param.8), kind=kOutput, calls=%fused_computation.81 | convolution fusion | flops 537395200 | bytes 3932160 | tf_op jit(solution)/shard_map/abik,blk->abil/dot_general | solution.py:30
  146.4 3.2 %fusion.46 = f32[2,4,256,256]{3,2,1,0:T(8,128)} fusion(bf16[4,2,256,256]{3,2,0,1:T(8,128)(2,1)S(1)} %fusion.19, bf16[4,4,256,256]{3,2,1,0:T(8,128)(2,1)} %param.7, bf16[2,4,256,256]{3,2,1,0:T(8,128)(2,1)} %param.8), kind=kOutput, calls=%fused_computation.83 | convolution fusion | flops 537395200 | bytes 3932160 | tf_op jit(solution)/shard_map/abik,blk->abil/dot_general | solution.py:30
  149.6 3.4 %fusion.48 = f32[2,4,256,256]{3,2,1,0:T(8,128)} fusion(bf16[1,4,256,256]{3,2,0,1:T(8,128)(2,1)} %collective-permute-done.6, bf16[4,1,256,256]{3,2,0,1:T(8,128)(2,1)} %collective-permute-done.5, bf16[4,2,256,256]{3,2,0,1:T(8,128)(2,1)S(1)} %fusion.19, bf16[4,1,256,256]{3,2,0,1:T(8,128)(2,1)} %collective-permute-done.4, bf16[4,4,256,256]{3,2,1,0:T(8,128)(2,1)} %param.7, ...), kind=kOutput, calls=%fused_computation.85 | convolution fusion | flops 541589504 | bytes 5505024 | tf_op jit(solution)/shard_map/abik,blk->abil/dot_general | solution.py:30
  153.0 9.7 %collective-permute-done.7 = bf16[1,4,256,256]{3,2,0,1:T(8,128)(2,1)} collective-permute-done((bf16[1,4,256,256]{3,2,0,1:T(8,128)(2,1)}, bf16[1,4,256,256]{3,2,0,1:T(8,128)(2,1)}, u32[]{:S(2)}, u32[]{:S(2)}) %collective-permute-start.7) | collective-permute-done | bytes 524320 | tf_op jit(solution)/shard_map/ppermute | solution.py:20
  162.7 7.0 %fusion.25 = (f32[]{:T(128)}, f32[]{:T(128)}, f32[]{:T(128)}, f32[]{:T(128)}, f32[]{:T(128)}, /*index=5*/f32[4,2,256,256]{3,2,0,1:T(8,128)}) fusion(bf16[4,2,256,256]{3,2,0,1:T(8,128)(2,1)S(1)} %fusion.1, bf16[4,2,256,256]{3,2,0,1:T(8,128)(2,1)S(1)} %fusion.19, bf16[2,4,256,256]{3,2,1,0:T(8,128)(2,1)} %param.8, ...), kind=kOutput, calls=%fused_computation.46 | convolution fusion | flops 550502400 | bytes 13894676 | tf_op jit(solution)/shard_map/abik,blk->abil/dot_general | solution.py:30
  169.7 21.3 %all-reduce.1 = (f32[]{:T(128)}, f32[]{:T(128)}, f32[]{:T(128)}, f32[]{:T(128)}, f32[]{:T(128)}) all-reduce(f32[]{:T(128)} %get-tuple-element.9, f32[]{:T(128)} %get-tuple-element.10, f32[]{:T(128)} %get-tuple-element.8, f32[]{:T(128)} %get-tuple-element.17, f32[]{:T(128)} %get-tuple-element.11), channel_id=1, replica_groups=mesh['lsec'=4,'rsec'=8] {'rsec'}, use_global_device_ids=true, to_apply=%region_23.0 | all-reduce | flops 5 | bytes 40 | tf_op jit(solution)/shard_map/psum | solution.py:77
  191.0 8.7 %all-reduce.4 = (f32[]{:T(128)}, f32[]{:T(128)}, f32[]{:T(128)}, f32[]{:T(128)}, f32[]{:T(128)}) all-reduce(f32[]{:T(128)} %get-tuple-element.24, f32[]{:T(128)} %get-tuple-element.25, f32[]{:T(128)} %get-tuple-element.26, f32[]{:T(128)} %get-tuple-element.27, f32[]{:T(128)} %get-tuple-element.28), channel_id=1, replica_groups=mesh['lsec'=4,'rsec'=8] {'lsec'}, use_global_device_ids=true, to_apply=%region_24.0 | all-reduce | flops 5 | bytes 40 | tf_op jit(solution)/shard_map/psum | solution.py:77
  205.0 2.2 fusion.24
  208.2 2.2 collective-permute-start.8
  214.6 2.2 pad_maximum_fusion.54
  216.7 4.1 %collective-permute-start.10 = (bf16[1,4,256,256]{3,2,0,1:T(8,128)(2,1)}, bf16[1,4,256,256]{3,2,0,1:T(8,128)(2,1)}, u32[]{:S(2)}, u32[]{:S(2)}) collective-permute-start(bf16[1,4,256,256]{3,2,0,1:T(8,128)(2,1)} %get-tuple-element.52), channel_id=1, source_target_pairs={{0,8},{8,16},{16,24},{1,9},{9,17},{17,25},{2,10},{10,18},{18,26},{... | collective-permute-start | bytes 1572872 | tf_op jit(solution)/shard_map/ppermute | solution.py:17
  220.9 3.0 %fusion.51 = f32[2,4,256,256]{3,2,1,0:T(8,128)} fusion(bf16[4,2,256,256]{3,2,0,1:T(8,128)(2,1)S(1)} %fusion.24, bf16[4,4,256,256]{3,2,1,0:T(8,128)(2,1)} %param.7, bf16[2,4,256,256]{3,2,1,0:T(8,128)(2,1)S(1)} %copy-done.2), kind=kOutput, calls=%fused_computation.88 | convolution fusion | flops 537395200 | bytes 3932160 | tf_op jit(solution)/shard_map/abik,blk->abil/dot_general | solution.py:30
  225.2 3.1 %fusion.53 = f32[2,4,256,256]{3,2,1,0:T(8,128)} fusion(bf16[4,2,256,256]{3,2,0,1:T(8,128)(2,1)S(1)} %fusion.24, bf16[4,4,256,256]{3,2,1,0:T(8,128)(2,1)} %param.7, bf16[2,4,256,256]{3,2,1,0:T(8,128)(2,1)S(1)} %copy-done.2), kind=kOutput, calls=%fused_computation.90 | convolution fusion | flops 537395200 | bytes 3932160 | tf_op jit(solution)/shard_map/abik,blk->abil/dot_general | solution.py:30
  228.3 3.3 %fusion.55 = f32[2,4,256,256]{3,2,1,0:T(8,128)} fusion(bf16[1,4,256,256]{3,2,0,1:T(8,128)(2,1)} %collective-permute-done.10, bf16[4,1,256,256]{3,2,0,1:T(8,128)(2,1)} %collective-permute-done.9, bf16[4,2,256,256]{3,2,0,1:T(8,128)(2,1)S(1)} %fusion.24, bf16[4,1,256,256]{3,2,0,1:T(8,128)(2,1)} %collective-permute-done.8, bf16[4,4,256,256]{3,2,1,0:T(8,128)(2,1)} %param.7, ...), kind=kOutput, calls=%fused_computation.92 | convolution fusion | flops 541589504 | bytes 5505024 | tf_op jit(solution)/shard_map/abik,blk->abil/dot_general | solution.py:30
  231.6 9.5 %collective-permute-done.11 = bf16[1,4,256,256]{3,2,0,1:T(8,128)(2,1)} collective-permute-done((bf16[1,4,256,256]{3,2,0,1:T(8,128)(2,1)}, bf16[1,4,256,256]{3,2,0,1:T(8,128)(2,1)}, u32[]{:S(2)}, u32[]{:S(2)}) %collective-permute-start.11) | collective-permute-done | bytes 524320 | tf_op jit(solution)/shard_map/ppermute | solution.py:20
  241.1 6.9 %fusion.34 = (f32[]{:T(128)}, f32[]{:T(128)}, f32[]{:T(128)}, f32[]{:T(128)}, f32[]{:T(128)}, /*index=5*/f32[4,2,256,256]{3,2,0,1:T(8,128)}) fusion(bf16[4,2,256,256]{3,2,0,1:T(8,128)(2,1)S(1)} %fusion.19, bf16[4,2,256,256]{3,2,0,1:T(8,128)(2,1)S(1)} %fusion.24, bf16[2,4,256,256]{3,2,1,0:T(8,128)(2,1)S(1)} %copy-done.2, ...), kind=kOutput, calls=%fused_computation.55 | convolution fusion | flops 550502400 | bytes 13894676 | tf_op jit(solution)/shard_map/abik,blk->abil/dot_general | solution.py:30
  248.1 22.0 %all-reduce = (f32[]{:T(128)}, f32[]{:T(128)}, f32[]{:T(128)}, f32[]{:T(128)}, f32[]{:T(128)}) all-reduce(f32[]{:T(128)} %get-tuple-element.5, f32[]{:T(128)} %get-tuple-element.6, f32[]{:T(128)} %get-tuple-element.4, f32[]{:T(128)} %get-tuple-element.18, f32[]{:T(128)} %get-tuple-element.7), channel_id=1, replica_groups=mesh['lsec'=4,'rsec'=8] {'rsec'}, use_global_device_ids=true, to_apply=%region_38.0 | all-reduce | flops 5 | bytes 40 | tf_op jit(solution)/shard_map/psum | solution.py:77
  270.1 8.7 %all-reduce.3 = (f32[]{:T(128)}, f32[]{:T(128)}, f32[]{:T(128)}, f32[]{:T(128)}, f32[]{:T(128)}) all-reduce(f32[]{:T(128)} %get-tuple-element.19, f32[]{:T(128)} %get-tuple-element.20, f32[]{:T(128)} %get-tuple-element.21, f32[]{:T(128)} %get-tuple-element.22, f32[]{:T(128)} %get-tuple-element.23), channel_id=1, replica_groups=mesh['lsec'=4,'rsec'=8] {'lsec'}, use_global_device_ids=true, to_apply=%region_39.0 | all-reduce | flops 5 | bytes 40 | tf_op jit(solution)/shard_map/psum | solution.py:77
  (42 shorter events, 21.9 us)
Async XLA Ops:
  47.4 13.1 %copy-start.1 = (bf16[4,4,256,256]{3,2,1,0:T(8,128)(2,1)S(1)}, bf16[4,4,256,256]{3,2,1,0:T(8,128)(2,1)}, u32[]{:S(2)}) copy-start(bf16[4,4,256,256]{3,2,1,0:T(8,128)(2,1)} %param.7) | copy-start | bytes 6291460
  47.4 2.9 %collective-permute-start = (bf16[4,1,256,256]{3,2,0,1:T(8,128)(2,1)S(1)}, bf16[4,1,256,256]{3,2,0,1:T(8,128)(2,1)S(1)}, u32[]{:S(2)}, u32[]{:S(2)}) collective-permute-start(bf16[4,1,256,256]{3,2,0,1:T(8,128)(2,1)S(1)} %get-tuple-element.61), channel_id=1, source_target_pairs={{0,1},{1,2},{2,3},{3,4},{4,5},{5,6},{6,7},{8,9},{9,10},{10,11},{11... | collective-permute-start | bytes 1572872 | tf_op jit(solution)/shard_map/ppermute | solution.py:17
  48.8 5.5 %collective-permute-start.1 = (bf16[4,1,256,256]{3,2,0,1:T(8,128)(2,1)S(1)}, bf16[4,1,256,256]{3,2,0,1:T(8,128)(2,1)S(1)}, u32[]{:S(2)}, u32[]{:S(2)}) collective-permute-start(bf16[4,1,256,256]{3,2,0,1:T(8,128)(2,1)S(1)} %get-tuple-element.62), channel_id=1, source_target_pairs={{1,0},{2,1},{3,2},{4,3},{5,4},{6,5},{7,6},{9,8},{10,9},{11,10},{12... | collective-permute-start | bytes 1572872 | tf_op jit(solution)/shard_map/ppermute | solution.py:20
  50.3 4.0 %copy-start.3 = (bf16[4,1,256,256]{3,2,0,1:T(8,128)(2,1)}, bf16[4,1,256,256]{3,2,0,1:T(8,128)(2,1)S(1)}, u32[]{:S(2)}) copy-start(bf16[4,1,256,256]{3,2,0,1:T(8,128)(2,1)S(1)} %collective-permute-done) | copy-start | bytes 1572868
  54.3 1.1 copy-start.4
  55.5 12.3 %collective-permute-start.2 = (bf16[1,4,256,256]{3,2,0,1:T(8,128)(2,1)}, bf16[1,4,256,256]{3,2,0,1:T(8,128)(2,1)}, u32[]{:S(2)}, u32[]{:S(2)}) collective-permute-start(bf16[1,4,256,256]{3,2,0,1:T(8,128)(2,1)} %get-tuple-element.56), channel_id=1, source_target_pairs={{0,8},{8,16},{16,24},{1,9},{9,17},{17,25},{2,10},{10,18},{18,26},{... | collective-permute-start | bytes 1572872 | tf_op jit(solution)/shard_map/ppermute | solution.py:17
  63.4 16.8 %collective-permute-start.3 = (bf16[1,4,256,256]{3,2,0,1:T(8,128)(2,1)}, bf16[1,4,256,256]{3,2,0,1:T(8,128)(2,1)}, u32[]{:S(2)}, u32[]{:S(2)}) collective-permute-start(bf16[1,4,256,256]{3,2,0,1:T(8,128)(2,1)} %get-tuple-element.55), channel_id=1, source_target_pairs={{8,0},{16,8},{24,16},{9,1},{17,9},{25,17},{10,2},{18,10},{26,18},{... | collective-permute-start | bytes 1572872 | tf_op jit(solution)/shard_map/ppermute | solution.py:20
  67.7 12.5 %copy-start.7 = (f32[4,2]{0,1:T(2,128)S(1)}, f32[4,2]{0,1:T(2,128)}, u32[]{:S(2)}) copy-start(f32[4,2]{0,1:T(2,128)} %param.9) | copy-start | bytes 100
  70.9 55.1 %copy-start = (bf16[4,2,256,256]{3,2,1,0:T(8,128)(2,1)S(1)}, bf16[4,2,256,256]{3,2,1,0:T(8,128)(2,1)}, u32[]{:S(2)}) copy-start(bf16[4,2,256,256]{3,2,1,0:T(8,128)(2,1)} %param.6) | copy-start | bytes 3145732
  128.1 4.5 %copy-start.5 = (s32[2]{0:T(128)S(1)}, s32[2]{0:T(128)}, u32[]{:S(2)}) copy-start(s32[2]{0:T(128)} %param.10) | copy-start | bytes 28
  128.1 5.7 %copy-start.6 = (s32[2]{0:T(128)S(1)}, s32[2]{0:T(128)}, u32[]{:S(2)}) copy-start(s32[2]{0:T(128)} %param.11) | copy-start | bytes 28
  129.1 6.6 %collective-permute-start.4 = (bf16[4,1,256,256]{3,2,0,1:T(8,128)(2,1)}, bf16[4,1,256,256]{3,2,0,1:T(8,128)(2,1)}, u32[]{:S(2)}, u32[]{:S(2)}) collective-permute-start(bf16[4,1,256,256]{3,2,0,1:T(8,128)(2,1)} %get-tuple-element.59), channel_id=1, source_target_pairs={{0,1},{1,2},{2,3},{3,4},{4,5},{5,6},{6,7},{8,9},{9,10},{10,11},{11... | collective-permute-start | bytes 1572872 | tf_op jit(solution)/shard_map/ppermute | solution.py:17
  131.2 4.5 %collective-permute-start.5 = (bf16[4,1,256,256]{3,2,0,1:T(8,128)(2,1)}, bf16[4,1,256,256]{3,2,0,1:T(8,128)(2,1)}, u32[]{:S(2)}, u32[]{:S(2)}) collective-permute-start(bf16[4,1,256,256]{3,2,0,1:T(8,128)(2,1)} %get-tuple-element.60), channel_id=1, source_target_pairs={{1,0},{2,1},{3,2},{4,3},{5,4},{6,5},{7,6},{9,8},{10,9},{11,10},{12... | collective-permute-start | bytes 1572872 | tf_op jit(solution)/shard_map/ppermute | solution.py:20
  137.9 11.7 %collective-permute-start.6 = (bf16[1,4,256,256]{3,2,0,1:T(8,128)(2,1)}, bf16[1,4,256,256]{3,2,0,1:T(8,128)(2,1)}, u32[]{:S(2)}, u32[]{:S(2)}) collective-permute-start(bf16[1,4,256,256]{3,2,0,1:T(8,128)(2,1)} %get-tuple-element.54), channel_id=1, source_target_pairs={{0,8},{8,16},{16,24},{1,9},{9,17},{17,25},{2,10},{10,18},{18,26},{... | collective-permute-start | bytes 1572872 | tf_op jit(solution)/shard_map/ppermute | solution.py:17
  145.1 17.5 %collective-permute-start.7 = (bf16[1,4,256,256]{3,2,0,1:T(8,128)(2,1)}, bf16[1,4,256,256]{3,2,0,1:T(8,128)(2,1)}, u32[]{:S(2)}, u32[]{:S(2)}) collective-permute-start(bf16[1,4,256,256]{3,2,0,1:T(8,128)(2,1)} %get-tuple-element.53), channel_id=1, source_target_pairs={{8,0},{16,8},{24,16},{9,1},{17,9},{25,17},{10,2},{18,10},{26,18},{... | collective-permute-start | bytes 1572872 | tf_op jit(solution)/shard_map/ppermute | solution.py:20
  208.2 12.7 %copy-start.2 = (bf16[2,4,256,256]{3,2,1,0:T(8,128)(2,1)S(1)}, bf16[2,4,256,256]{3,2,1,0:T(8,128)(2,1)}, u32[]{:S(2)}) copy-start(bf16[2,4,256,256]{3,2,1,0:T(8,128)(2,1)} %param.8) | copy-start | bytes 3145732
  208.2 5.5 %collective-permute-start.8 = (bf16[4,1,256,256]{3,2,0,1:T(8,128)(2,1)}, bf16[4,1,256,256]{3,2,0,1:T(8,128)(2,1)}, u32[]{:S(2)}, u32[]{:S(2)}) collective-permute-start(bf16[4,1,256,256]{3,2,0,1:T(8,128)(2,1)} %get-tuple-element.57), channel_id=1, source_target_pairs={{0,1},{1,2},{2,3},{3,4},{4,5},{5,6},{6,7},{8,9},{9,10},{10,11},{11... | collective-permute-start | bytes 1572872 | tf_op jit(solution)/shard_map/ppermute | solution.py:17
  210.4 4.1 %collective-permute-start.9 = (bf16[4,1,256,256]{3,2,0,1:T(8,128)(2,1)}, bf16[4,1,256,256]{3,2,0,1:T(8,128)(2,1)}, u32[]{:S(2)}, u32[]{:S(2)}) collective-permute-start(bf16[4,1,256,256]{3,2,0,1:T(8,128)(2,1)} %get-tuple-element.58), channel_id=1, source_target_pairs={{1,0},{2,1},{3,2},{4,3},{5,4},{6,5},{7,6},{9,8},{10,9},{11,10},{12... | collective-permute-start | bytes 1572872 | tf_op jit(solution)/shard_map/ppermute | solution.py:20
  216.7 11.6 %collective-permute-start.10 = (bf16[1,4,256,256]{3,2,0,1:T(8,128)(2,1)}, bf16[1,4,256,256]{3,2,0,1:T(8,128)(2,1)}, u32[]{:S(2)}, u32[]{:S(2)}) collective-permute-start(bf16[1,4,256,256]{3,2,0,1:T(8,128)(2,1)} %get-tuple-element.52), channel_id=1, source_target_pairs={{0,8},{8,16},{16,24},{1,9},{9,17},{17,25},{2,10},{10,18},{18,26},{... | collective-permute-start | bytes 1572872 | tf_op jit(solution)/shard_map/ppermute | solution.py:17
  223.9 17.2 %collective-permute-start.11 = (bf16[1,4,256,256]{3,2,0,1:T(8,128)(2,1)}, bf16[1,4,256,256]{3,2,0,1:T(8,128)(2,1)}, u32[]{:S(2)}, u32[]{:S(2)}) collective-permute-start(bf16[1,4,256,256]{3,2,0,1:T(8,128)(2,1)} %get-tuple-element.51), channel_id=1, source_target_pairs={{8,0},{16,8},{24,16},{9,1},{17,9},{25,17},{10,2},{18,10},{26,18},{... | collective-permute-start | bytes 1572872 | tf_op jit(solution)/shard_map/ppermute | solution.py:20
